TPU v7x, 32 devices: a whole 2x2x4 slice. The times are simulated.
32 devices in a mesh: row: 8 (over z, x), col: 4 (over y, core).
Axes of the slice: x: 2, y: 2, z: 4, core: 2. Of those that a mesh axis runs over, the one named last changes fastest.
Arguments:
- diagonal_inverses: bfloat16 [24, 2048, 2048], P('row', 'col'), may hold values from -0.125 to 0.125
- column_basis: bfloat16 [24, 2048, 256], P('row', 'col'), may hold values from -6 to 6
- row_basis: bfloat16 [24, 2048, 256], P('row', 'col'), may hold values from -0.125 to 0.125
- transfer: float32 [24, 256, 256], P('row', 'col'), may hold values from -0.375 to 0.375
- coupling: float32 [24, 256, 256], P('row', 'col'), may hold values from -6 to 6
- ranks: int32 [24], P('row'), may hold values from 128 to 256, as said below
Outputs:
- merged: float32 [24, 256, 256], P('row', 'col')
- parent_skeleton: float32 [24, 256, 256], P('row', 'col')
Inputs may be any that keep to these rules, and one draw needn't show every extreme that they name: `ranks`: each rank is 128 or 256; both occur in every draw.
All inputs are finite; a program needn't handle non-finite values.
Results may differ from a plain program's by a relative error of at most 0.0021.
Values may be sent and summed in bfloat16 or wider, within the bound.
A program may use at most 64 MiB of HBM per device.

v0:
```python
import jax
import jax.numpy as jnp
from jax import lax
from jax.sharding import PartitionSpec as P

BIT = 2


def swapped(block, axis, bit):
    count = lax.axis_size(axis)
    route = []
    for low in range(count):
        high = low | 1 << bit
        if high != low and high < count:
            route += [(low, high), (high, low)]
    return lax.ppermute(block, axis, route)


def shards(diagonal_inverses, column_basis, row_basis, transfer, coupling, ranks):
    rank_width = transfer.shape[2]
    part_rows = transfer.shape[1]
    highest = lax.Precision.HIGHEST
    live_cols = jnp.arange(rank_width, dtype=jnp.int32)[None, :] < ranks[:, None]
    left_factor_basis = jnp.where(live_cols[:, None, :], column_basis, jnp.zeros_like(column_basis))
    right_factor_basis = jnp.where(live_cols[:, None, :], row_basis, jnp.zeros_like(row_basis))
    eliminated_part = jnp.einsum(
        "nmp,npr->nmr",
        diagonal_inverses,
        lax.all_gather(left_factor_basis, "col", axis=1, tiled=True),
        preferred_element_type=jnp.float32,
    ).astype(jnp.bfloat16)
    skeleton = jnp.transpose(
        lax.psum_scatter(
            jnp.einsum(
                "hgp,hgd->phd",
                right_factor_basis,
                eliminated_part,
                preferred_element_type=jnp.float32,
            ),
            "col",
            scatter_dimension=0,
            tiled=True,
        ),
        (1, 0, 2),
    )
    offset_rows = lax.axis_index("col") * part_rows
    active_rows = lax.dynamic_slice_in_dim(live_cols, offset_rows, part_rows, 1)
    masked = transfer * active_rows[:, :, None].astype(jnp.float32)
    masked_sib = swapped(masked, "row", BIT)
    complete_local_block, whole_sib = (
        lax.all_gather(masked, "col", axis=1, tiled=True),
        lax.all_gather(masked_sib, "col", axis=1, tiled=True),
    )
    merged = jnp.einsum("nij,njk->nik", skeleton, complete_local_block, precision=highest)
    merged = merged + jnp.einsum("nij,njk->nik", coupling, whole_sib, precision=highest)
    own_term = jnp.transpose(
        lax.psum_scatter(
            jnp.einsum("nji,njk->ink", masked, merged, precision=highest),
            "col",
            scatter_dimension=0,
            tiled=True,
        ),
        (1, 0, 2),
    )
    parent = own_term + swapped(own_term, "row", BIT)
    return (merged, parent)


def solution(mesh):
    placed = (
        P("row", "col", None),
        P("row", "col", None),
        P("row", "col", None),
        P("row", "col", None),
        P("row", "col", None),
        P("row"),
    )
    return jax.shard_map(
        shards,
        mesh=mesh,
        in_specs=placed,
        out_specs=(P("row", "col", None), P("row", "col", None)),
        check_vma=False,
    )
```

profile of v0, /device:TPU:0, one launch (start us, length us, event | category | flops | bytes accessed | tf_op | source)
XLA Modules:
  0.0 138.4 jit_solution(1713739336658735654)
XLA Ops:
  7.2 0.8 iota_compare_fusion
  8.0 2.1 %broadcast_select_fusion = bf16[3,512,256]{2,1,0:T(8,128)(2,1)} fusion(bf16[3,512,256]{2,1,0:T(8,128)(2,1)} %param.7, pred[3,256]{1,0:T(4,128)(4,1)S(1)} %iota_compare_fusion), kind=kLoop, calls=%fused_computation.7 | loop fusion | flops 393216 | bytes 1573632 | tf_op jit(solution)/shard_map/jit(_where)/select_n | solution.py:24
  10.1 0.0 reduce-scatter.2.cloned.1.call-start
  10.2 31.3 %all-gather.2.cloned.1.call-done = bf16[3,2048,256]{2,1,0:T(8,128)(2,1)} async-done(((bf16[3,512,256]{2,1,0:T(8,128)(2,1)}), bf16[3,2048,256]{2,1,0:T(8,128)(2,1)}) %all-gather.2.cloned.1.call-update) | async-done | bytes 3145744 | tf_op jit(solution)/shard_map/all_gather | solution.py:29
  41.5 7.1 %convolution_bitcast_fusion = f32[256,3,256]{2,0,1:T(8,128)} fusion(bf16[3,2048,256]{2,1,0:T(8,128)(2,1)} %all-gather.2.cloned.1.call-done, bf16[3,512,2048]{2,1,0:T(8,128)(2,1)} %param.6, bf16[3,512,256]{2,1,0:T(8,128)(2,1)} %param.8, pred[3,256]{1,0:T(4,128)(4,1)S(1)} %iota_compare_fusion), kind=kOutput, calls=%fused_computation.1 | convolution fusion | flops 1812725760 | bytes 11010816 | tf_op jit(solution)/shard_map/hgp,hgd->phd/dot_general | solution.py:34
  48.6 0.0 all-reduce.3.cloned.1.call-start
  48.7 0.1 dynamic-slice_convert_fusion
  48.8 0.1 broadcast_multiply_fusion
  48.9 2.5 %collective-permute-start = (f32[3,64,256]{2,1,0:T(8,128)S(1)}, f32[3,64,256]{2,1,0:T(8,128)S(1)}, u32[]{:S(2)}, u32[]{:S(2)}) collective-permute-start(f32[3,64,256]{2,1,0:T(8,128)S(1)} %broadcast_multiply_fusion), channel_id=1, source_target_pairs={{0,16},{16,0},{4,20},{20,4},{8,24},{24,8},{12,28},{28,12},{1,17},{... | collective-permute-start | bytes 589832 | tf_op jit(solution)/shard_map/ppermute | solution.py:16
  51.3 8.3 %all_gather.10 = f32[3,256,256]{2,1,0:T(8,128)S(1)} all-gather(f32[3,64,256]{2,1,0:T(8,128)S(1)} %broadcast_multiply_fusion), channel_id=1, replica_groups=mesh['row'=8,'col'=4] {'col'}, dimensions={1}, use_global_device_ids=true | all-gather | bytes 983040 | tf_op jit(solution)/shard_map/all_gather | solution.py:51
  59.6 1.4 %collective-permute-done = f32[3,64,256]{2,1,0:T(8,128)S(1)} collective-permute-done((f32[3,64,256]{2,1,0:T(8,128)S(1)}, f32[3,64,256]{2,1,0:T(8,128)S(1)}, u32[]{:S(2)}, u32[]{:S(2)}) %collective-permute-start) | collective-permute-done | bytes 196640 | tf_op jit(solution)/shard_map/ppermute | solution.py:16
  61.1 10.0 %all_gather.11 = f32[3,256,256]{2,1,0:T(8,128)S(1)} all-gather(f32[3,64,256]{2,1,0:T(8,128)S(1)} %collective-permute-done), channel_id=1, replica_groups=mesh['row'=8,'col'=4] {'col'}, dimensions={1}, use_global_device_ids=true | all-gather | bytes 983040 | tf_op jit(solution)/shard_map/all_gather | solution.py:52
  71.1 2.1 %reduce-scatter.2.cloned.1.call-done = f32[64,3,256]{2,0,1:T(8,128)} async-done(((f32[256,3,256]{2,0,1:T(8,128)}), f32[64,3,256]{2,0,1:T(8,128)}) %reduce-scatter.2.cloned.1.call-update) | async-done | bytes 196624 | tf_op jit(solution)/shard_map/reduce_scatter | solution.py:33
  73.2 1.5 %fusion.4 = f32[3,64,256]{2,1,0:T(8,128)S(1)} fusion(f32[3,256,256]{2,1,0:T(8,128)S(1)} %all_gather.10, f32[64,3,256]{2,0,1:T(8,128)} %reduce-scatter.2.cloned.1.call-done), kind=kOutput, calls=%fused_computation.10 | convolution fusion | flops 150994944 | bytes 1179648 | tf_op jit(solution)/shard_map/nij,njk->nik/dot_general | solution.py:54
  74.7 0.6 fusion
  75.4 0.8 convolution_bitcast_fusion.1
  76.2 1.4 copy.9
  77.6 0.6 dynamic-slice
  78.8 36.0 %all-reduce.3.cloned.1.call-done = f32[256,3,256]{2,1,0:T(4,128)} async-done(((f32[256,3,256]{2,1,0:T(4,128)}), f32[256,3,256]{2,1,0:T(4,128)}) %all-reduce.3.cloned.1.call-update) | async-done | bytes 786448
  114.8 1.0 dynamic-slice_bitcast_fusion
  115.8 2.5 %collective-permute-start.1 = (f32[3,64,256]{2,0,1:T(4,128)S(1)}, f32[3,64,256]{2,0,1:T(4,128)S(1)}, u32[]{:S(2)}, u32[]{:S(2)}) collective-permute-start(f32[3,64,256]{2,0,1:T(4,128)S(1)} %dynamic-slice_bitcast_fusion), channel_id=1, source_target_pairs={{0,16},{16,0},{4,20},{20,4},{8,24},{24,8},{12,28},{28,12},{1,17},{... | collective-permute-start | bytes 589832 | tf_op jit(solution)/shard_map/ppermute | solution.py:16
  118.3 11.8 %collective-permute-done.1 = f32[3,64,256]{2,0,1:T(4,128)S(1)} collective-permute-done((f32[3,64,256]{2,0,1:T(4,128)S(1)}, f32[3,64,256]{2,0,1:T(4,128)S(1)}, u32[]{:S(2)}, u32[]{:S(2)}) %collective-permute-start.1) | collective-permute-done | bytes 196640 | tf_op jit(solution)/shard_map/ppermute | solution.py:16
  130.1 1.0 fusion.14
  131.1 0.7 copy.10
  (12 shorter events, 0.1 us)
Async XLA Ops:
  7.2 67.6 %copy-start = (f32[3,64,256]{2,1,0:T(8,128)S(1)}, f32[3,64,256]{2,1,0:T(8,128)}, u32[]{:S(2)}) copy-start(f32[3,64,256]{2,1,0:T(8,128)} %param.10) | copy-start | bytes 589828
  7.2 34.3 %all-gather.2.cloned.1.call-start = ((), (), s32[]{:S(2)}) async-start(), calls=%async_computation.1 | async-start | bytes 3932160 | tf_op jit(solution)/shard_map/all_gather | solution.py:29
  10.1 38.7 %copy-start.2 = (f32[3,64,256]{2,1,0:T(8,128)S(1)}, f32[3,64,256]{2,1,0:T(8,128)}, u32[]{:S(2)}) copy-start(f32[3,64,256]{2,1,0:T(8,128)} %param.9) | copy-start | bytes 589828
  10.1 63.1 %reduce-scatter.2.cloned.1.call-start = ((), (), s32[]{:S(2)}) async-start(), calls=%async_computation.2 | async-start | bytes 983040 | tf_op jit(solution)/shard_map/reduce_scatter | solution.py:33
  48.6 66.2 %all-reduce.3.cloned.1.call-start = ((), (), s32[]{:S(2)}) async-start(), calls=%async_computation.3 | async-start | bytes 2097152
  48.9 12.2 %collective-permute-start = (f32[3,64,256]{2,1,0:T(8,128)S(1)}, f32[3,64,256]{2,1,0:T(8,128)S(1)}, u32[]{:S(2)}, u32[]{:S(2)}) collective-permute-start(f32[3,64,256]{2,1,0:T(8,128)S(1)} %broadcast_multiply_fusion), channel_id=1, source_target_pairs={{0,16},{16,0},{4,20},{20,4},{8,24},{24,8},{12,28},{28,12},{1,17},{... | collective-permute-start | bytes 589832 | tf_op jit(solution)/shard_map/ppermute | solution.py:16
  71.1 6.5 %copy-start.3 = (u32[32]{0:T(128)S(1)}, u32[32]{0:T(128)}, u32[]{:S(2)}) copy-start(u32[32]{0:T(128)} %constant.20) | copy-start | bytes 388
  75.4 56.5 %copy-start.1 = (f32[3,64,256]{2,1,0:T(8,128)}, f32[3,64,256]{2,1,0:T(8,128)S(1)}, u32[]{:S(2)}) copy-start(f32[3,64,256]{2,1,0:T(8,128)S(1)} %fusion) | copy-start | bytes 589828
  115.8 14.3 %collective-permute-start.1 = (f32[3,64,256]{2,0,1:T(4,128)S(1)}, f32[3,64,256]{2,0,1:T(4,128)S(1)}, u32[]{:S(2)}, u32[]{:S(2)}) collective-permute-start(f32[3,64,256]{2,0,1:T(4,128)S(1)} %dynamic-slice_bitcast_fusion), channel_id=1, source_target_pairs={{0,16},{16,0},{4,20},{20,4},{8,24},{24,8},{12,28},{28,12},{1,17},{... | collective-permute-start | bytes 589832 | tf_op jit(solution)/shard_map/ppermute | solution.py:16
Sparse Core Ops, SparseCore 0:
  10.2 31.2 all-gather.1
  48.7 24.3 reduce-scatter.1
  77.7 37.0 all-reduce.2
where the time goes:
time: 139 us; the launch traced here: 138 us
  waiting for transfers between devices  82.7 us (59%)
  blocking collectives  18.3 us (13%)
  between operations  14.5 us (10%)
  matrix products  10.1 us (7%)
  starting transfers between devices  5.07 us (4%)
  other arithmetic  4.03 us (3%)
  local copies, waits for them, and re-layouts  3.68 us (3%)
    unnamed x4, waiting for transfers between devices  36 us
    all_gather x1, waiting for transfers between devices, shards(): lax.all_gather(left_factor_basis, 'col', axis=1, tiled=True)  31.3 us
    ppermute x2, waiting for transfers between devices, swapped(): return lax.ppermute(block, axis, route)  13.3 us
    all_gather x1, blocking collectives, shards(): lax.all_gather(masked_sib, 'col', axis=1, tiled=True)  9.98 us
    all_gather x1, blocking collectives, shards(): lax.all_gather(masked, 'col', axis=1, tiled=True)  8.3 us
    dot_general x1, matrix products, shards(): jnp.einsum('hgp,hgd->phd', right_factor_basis, eliminated_part, preferred...  7.12 us
    ppermute x2, starting transfers between devices, swapped(): return lax.ppermute(block, axis, route)  4.94 us
  transfers between devices with their start and end apart: 5, of which 5 were waited for; matrix products, arithmetic and copies ran while one was open for 1% of the time, Pallas kernels for 0%

commit v1 on v0

--- a/solution.py
+++ b/solution.py
@@ -4,6 +4,12 @@
 from jax.sharding import PartitionSpec as P
 
 BIT = 2
+
+
+def gather_by_exchange(x, axis, dim):
+    size = lax.axis_size(axis)
+    repeats = [size if d == dim else 1 for d in range(x.ndim)]
+    return lax.all_to_all(jnp.tile(x, repeats), axis, split_axis=dim, concat_axis=dim, tiled=True)
 
 
 def swapped(block, axis, bit):
@@ -26,7 +32,7 @@
     eliminated_part = jnp.einsum(
         "nmp,npr->nmr",
         diagonal_inverses,
-        lax.all_gather(left_factor_basis, "col", axis=1, tiled=True),
+        gather_by_exchange(left_factor_basis, "col", 1),
         preferred_element_type=jnp.float32,
     ).astype(jnp.bfloat16)
     skeleton = jnp.transpose(

time: 139 us -> 161 us (1.16)
  blocking collectives: 18.3 us -> 68.3 us
  waiting for transfers between devices: 82.7 us -> 53.1 us
  local copies, waits for them, and re-layouts: 3.68 us -> 5.45 us
    all_to_all x0 -> x1, blocking collectives: none -> 52.4 us  [gather_by_exchange(): lax.all_to_all(jnp.tile(x, repeats), axis, split_axis=dim, concat_axis=di...]
    all_gather x1 -> x0, waiting for transfers between devices: 31.3 us -> none  [shards(): lax.all_gather(left_factor_basis, 'col', axis=1, tiled=True)]
    reduce_scatter x1, waiting for transfers between devices: 2.13 us -> 3.96 us  [shards(): lax.psum_scatter(jnp.einsum('hgp,hgd->phd', right_factor_basis, eliminate...]
    all_gather x1, blocking collectives: 9.98 us -> 8.32 us  [shards(): lax.all_gather(masked_sib, 'col', axis=1, tiled=True)]
    unnamed x4 -> x3, waiting for transfers between devices: 36 us -> 36.2 us
  transfers between devices with their start and end apart: 5 -> 4, of which waited for: 5 -> 4; matrix products, arithmetic and copies ran while one was open for 1% -> 0% of each run, Pallas kernels for 0% -> 0%
where the time goes in v1:
time: 161 us
  blocking collectives  68.3 us (42%)
  waiting for transfers between devices  53.1 us (33%)
  between operations  14.8 us (9%)
  matrix products  10.4 us (6%)
  starting transfers between devices  5.92 us (4%)
  local copies, waits for them, and re-layouts  5.45 us (3%)
  other arithmetic  3.15 us (2%)
    all_to_all x1, blocking collectives, gather_by_exchange(): lax.all_to_all(jnp.tile(x, repeats), axis, split_axis=dim, concat_axis=di...  52.4 us
    unnamed x3, waiting for transfers between devices  36.2 us
    ppermute x2, waiting for transfers between devices, swapped(): return lax.ppermute(block, axis, route)  13 us
    all_gather x1, blocking collectives, shards(): lax.all_gather(masked_sib, 'col', axis=1, tiled=True)  8.32 us
    all_gather x1, blocking collectives, shards(): lax.all_gather(masked, 'col', axis=1, tiled=True)  7.53 us
    dot_general x1, matrix products, shards(): jnp.einsum('hgp,hgd->phd', right_factor_basis, eliminated_part, preferred...  7.38 us
    ppermute x2, starting transfers between devices, swapped(): return lax.ppermute(block, axis, route)  5.84 us
    reduce_scatter x1, waiting for transfers between devices, shards(): lax.psum_scatter(jnp.einsum('hgp,hgd->phd', right_factor_basis, eliminate...  3.96 us
  transfers between devices with their start and end apart: 4, of which 4 were waited for; matrix products, arithmetic and copies ran while one was open for 0% of the time, Pallas kernels for 0%

profile of v1, /device:TPU:0, one launch (start us, length us, event | category | flops | bytes accessed | tf_op | source)
XLA Modules:
  0.0 161.1 jit_solution(7371309907231867414)
XLA Ops:
  7.2 0.8 iota_compare_fusion
  8.0 1.2 broadcast_select_fusion
  9.2 0.7 copy.9
  9.9 1.1 tile.4
  11.0 52.4 %all_to_all.5 = bf16[3,2048,256]{2,0,1:T(4,128)(2,1)} all-to-all(bf16[3,2048,256]{2,0,1:T(4,128)(2,1)S(1)} %bitcast.23), channel_id=1, replica_groups=mesh['row'=8,'col'=4] {'col'}, dimensions={1} | all-to-all | bytes 6291456 | tf_op jit(solution)/shard_map/all_to_all | solution.py:12
  63.4 7.4 %convolution_bitcast_fusion = f32[256,3,256]{2,0,1:T(8,128)} fusion(bf16[3,512,2048]{2,1,0:T(8,128)(2,1)} %param.6, bf16[3,2048,256]{2,0,1:T(4,128)(2,1)} %all_to_all.5, bf16[3,512,256]{2,1,0:T(8,128)(2,1)S(1)} %copy-done.3, pred[3,256]{1,0:T(4,128)(4,1)S(1)} %iota_compare_fusion), kind=kOutput, calls=%fused_computation.3 | convolution fusion | flops 1812725760 | bytes 11010816 | tf_op jit(solution)/shard_map/hgp,hgd->phd/dot_general | solution.py:40
  70.9 0.1 dynamic-slice_convert_fusion
  71.0 0.1 broadcast_multiply_fusion
  71.1 3.4 %collective-permute-start = (f32[3,64,256]{2,1,0:T(8,128)S(1)}, f32[3,64,256]{2,1,0:T(8,128)S(1)}, u32[]{:S(2)}, u32[]{:S(2)}) collective-permute-start(f32[3,64,256]{2,1,0:T(8,128)S(1)} %broadcast_multiply_fusion), channel_id=1, source_target_pairs={{0,16},{16,0},{4,20},{20,4},{8,24},{24,8},{12,28},{28,12},{1,17},{... | collective-permute-start | bytes 589832 | tf_op jit(solution)/shard_map/ppermute | solution.py:22
  74.4 7.5 %all_gather.6 = f32[3,256,256]{2,1,0:T(8,128)S(1)} all-gather(f32[3,64,256]{2,1,0:T(8,128)S(1)} %broadcast_multiply_fusion), channel_id=1, replica_groups=mesh['row'=8,'col'=4] {'col'}, dimensions={1}, use_global_device_ids=true | all-gather | bytes 983040 | tf_op jit(solution)/shard_map/all_gather | solution.py:57
  82.0 1.2 collective-permute-done
  83.2 8.3 %all_gather.7 = f32[3,256,256]{2,1,0:T(8,128)S(1)} all-gather(f32[3,64,256]{2,1,0:T(8,128)S(1)} %collective-permute-done), channel_id=1, replica_groups=mesh['row'=8,'col'=4] {'col'}, dimensions={1}, use_global_device_ids=true | all-gather | bytes 983040 | tf_op jit(solution)/shard_map/all_gather | solution.py:58
  91.5 4.0 %reduce-scatter.2.cloned.1.call-done = f32[64,3,256]{2,0,1:T(8,128)} async-done(((f32[256,3,256]{2,0,1:T(8,128)}), f32[64,3,256]{2,0,1:T(8,128)}) %reduce-scatter.2.cloned.1.call-update) | async-done | bytes 196624 | tf_op jit(solution)/shard_map/reduce_scatter | solution.py:39
  95.5 1.5 fusion.11
  97.0 0.6 fusion.7
  97.6 0.8 convolution_bitcast_fusion.1
  98.5 1.4 copy.10
  99.9 0.6 dynamic-slice
  101.1 36.1 %all-reduce.3.cloned.1.call-done = f32[256,3,256]{2,1,0:T(4,128)} async-done(((f32[256,3,256]{2,1,0:T(4,128)}), f32[256,3,256]{2,1,0:T(4,128)}) %all-reduce.3.cloned.1.call-update) | async-done | bytes 786448
  137.3 1.0 dynamic-slice_bitcast_fusion
  138.3 2.5 %collective-permute-start.1 = (f32[3,64,256]{2,0,1:T(4,128)S(1)}, f32[3,64,256]{2,0,1:T(4,128)S(1)}, u32[]{:S(2)}, u32[]{:S(2)}) collective-permute-start(f32[3,64,256]{2,0,1:T(4,128)S(1)} %dynamic-slice_bitcast_fusion), channel_id=1, source_target_pairs={{0,16},{16,0},{4,20},{20,4},{8,24},{24,8},{12,28},{28,12},{1,17},{... | collective-permute-start | bytes 589832 | tf_op jit(solution)/shard_map/ppermute | solution.py:22
  140.7 11.8 %collective-permute-done.1 = f32[3,64,256]{2,0,1:T(4,128)S(1)} collective-permute-done((f32[3,64,256]{2,0,1:T(4,128)S(1)}, f32[3,64,256]{2,0,1:T(4,128)S(1)}, u32[]{:S(2)}, u32[]{:S(2)}) %collective-permute-start.1) | collective-permute-done | bytes 196640 | tf_op jit(solution)/shard_map/ppermute | solution.py:22
  152.5 1.0 fusion.20
  153.6 0.7 copy.11
  (14 shorter events, 0.1 us)
Async XLA Ops:
  7.2 89.8 %copy-start = (f32[3,64,256]{2,1,0:T(8,128)S(1)}, f32[3,64,256]{2,1,0:T(8,128)}, u32[]{:S(2)}) copy-start(f32[3,64,256]{2,1,0:T(8,128)} %param.10) | copy-start | bytes 589828
  7.2 88.3 %reduce-scatter.2.cloned.1.call-start = ((), (), s32[]{:S(2)}) async-start(), calls=%async_computation.2 | async-start | bytes 983040 | tf_op jit(solution)/shard_map/reduce_scatter | solution.py:39
  11.0 52.5 %copy-start.3 = (bf16[3,512,256]{2,1,0:T(8,128)(2,1)S(1)}, bf16[3,512,256]{2,1,0:T(8,128)(2,1)}, u32[]{:S(2)}) copy-start(bf16[3,512,256]{2,1,0:T(8,128)(2,1)} %param.8) | copy-start | bytes 2359300
  63.4 7.5 %copy-start.2 = (f32[3,64,256]{2,1,0:T(8,128)S(1)}, f32[3,64,256]{2,1,0:T(8,128)}, u32[]{:S(2)}) copy-start(f32[3,64,256]{2,1,0:T(8,128)} %param.9) | copy-start | bytes 589828
  70.8 66.4 %all-reduce.3.cloned.1.call-start = ((), (), s32[]{:S(2)}) async-start(), calls=%async_computation.3 | async-start | bytes 2097152
  71.1 28.8 %copy-start.4 = (u32[32]{0:T(128)S(1)}, u32[32]{0:T(128)}, u32[]{:S(2)}) copy-start(u32[32]{0:T(128)} %constant.20) | copy-start | bytes 388
  71.1 12.1 %collective-permute-start = (f32[3,64,256]{2,1,0:T(8,128)S(1)}, f32[3,64,256]{2,1,0:T(8,128)S(1)}, u32[]{:S(2)}, u32[]{:S(2)}) collective-permute-start(f32[3,64,256]{2,1,0:T(8,128)S(1)} %broadcast_multiply_fusion), channel_id=1, source_target_pairs={{0,16},{16,0},{4,20},{20,4},{8,24},{24,8},{12,28},{28,12},{1,17},{... | collective-permute-start | bytes 589832 | tf_op jit(solution)/shard_map/ppermute | solution.py:22
  97.6 56.7 %copy-start.1 = (f32[3,64,256]{2,1,0:T(8,128)}, f32[3,64,256]{2,1,0:T(8,128)S(1)}, u32[]{:S(2)}) copy-start(f32[3,64,256]{2,1,0:T(8,128)S(1)} %fusion.7) | copy-start | bytes 589828
  138.3 14.3 %collective-permute-start.1 = (f32[3,64,256]{2,0,1:T(4,128)S(1)}, f32[3,64,256]{2,0,1:T(4,128)S(1)}, u32[]{:S(2)}, u32[]{:S(2)}) collective-permute-start(f32[3,64,256]{2,0,1:T(4,128)S(1)} %dynamic-slice_bitcast_fusion), channel_id=1, source_target_pairs={{0,16},{16,0},{4,20},{20,4},{8,24},{24,8},{12,28},{28,12},{1,17},{... | collective-permute-start | bytes 589832 | tf_op jit(solution)/shard_map/ppermute | solution.py:22
Sparse Core Ops, SparseCore 0:
  70.9 24.4 reduce-scatter.1
  100.0 37.2 all-reduce.2
